TPU v7x, 256 devices: a whole 4x4x8 slice. The times are simulated.
256 devices in a mesh: dp: 2 (over x_lo), expert: 8 (over z), shard: 16 (over x_hi, y, core).
Axes of the slice: x: 4 (x_hi: 2, x_lo: 2; x = x_hi * 2 + x_lo), y: 4, z: 8, core: 2. Of those that a mesh axis runs over, the one named last changes fastest.
Arguments:
- tokens: bfloat16 [2048, 6144], P(('dp', 'expert', 'shard')), may hold values from -6 to 6
- gate_up_weight: bfloat16 [8, 2, 8192, 6144], P(None, None, ('dp', 'expert', 'shard')), may hold values from -0.078125 to 0.078125
- down_weight: bfloat16 [8, 8192, 6144], P(None, ('dp', 'expert', 'shard')), may hold values from -0.0625 to 0.0625
- expert_ids: int32 [2048, 2], P(('dp', 'expert', 'shard')), may hold values from 0 to 7, as said below
- slot_ids: int32 [2048, 2], P(('dp', 'expert', 'shard')), may hold values from 0 to 3, as said below
- gate_values: float32 [2048, 2], P(('dp', 'expert', 'shard')), may hold values from 0.1 to 1
- old_place: int32 [8], replicated, may hold values from 0 to 7, each once
- new_place: int32 [8], replicated, may hold values from 0 to 7, each once
Outputs:
- mixed_out: bfloat16 [2048, 6144], P(('dp', 'expert', 'shard'))
Inputs may be any that keep to these rules, and one draw needn't show every extreme that they name: `expert_ids`: each token names 2 different experts; among the 8 tokens of one block no expert is named more than 4 times, and one expert is named exactly 4 times in every block. `slot_ids`: within one block, two choices that name the same expert have different slots. `old_place`: each expert number appears once. `new_place`: each expert number appears once.
All inputs are finite; a program needn't handle non-finite values.
Results may differ from a plain program's by a relative error of at most 0.02.
Values may be sent and summed in bfloat16 or wider, within the bound.
A program may use at most 128 MiB of HBM per device.

v0:
```python
import jax
import jax.numpy as jnp
from jax import lax
from jax.sharding import PartitionSpec as P


def placement_order(old_place, new_place):
    slot_total = old_place.shape[0]
    matches = (new_place[:, None] == old_place[None, :]).astype(jnp.int32)
    return jnp.sum(matches * jnp.arange(slot_total, dtype=jnp.int32)[None, :], axis=1)


def swiglu_rows(row_block, pair_weight):
    gate_up = jnp.einsum("rd,gud->rgu", row_block, pair_weight, preferred_element_type=jnp.float32)
    return (jax.nn.silu(gate_up[:, 0]) * gate_up[:, 1]).astype(jnp.bfloat16)


def local(
    tokens, gate_up_weight, down_weight, expert_ids, slot_ids, gate_values, old_place, new_place
):
    experts = gate_up_weight.shape[0]
    sliver = gate_up_weight.shape[2]
    model_width = tokens.shape[1]
    tok_rows = tokens.shape[0]
    choices_per_token = expert_ids.shape[1]
    capacity = 2 * tok_rows * choices_per_token // experts
    cell_count = experts * capacity
    data_ways = lax.axis_size("dp")
    slot_order = placement_order(old_place, new_place)
    cell_ids = expert_ids * capacity + slot_ids
    cell_range = jnp.arange(cell_count, dtype=jnp.int32)
    cell_hits = (cell_ids[:, :, None] == cell_range[None, None, :]).astype(jnp.float32)
    token_picks = jnp.sum(cell_hits, axis=1)
    dispatched = jnp.dot(
        token_picks.T.astype(jnp.bfloat16), tokens, preferred_element_type=jnp.float32
    ).astype(jnp.bfloat16)
    received = lax.all_to_all(
        dispatched.reshape(experts, capacity, model_width),
        "expert",
        split_axis=0,
        concat_axis=0,
        tiled=True,
    )
    own_rows = received.reshape(cell_count, model_width)
    sectioned_in = gate_up_weight.reshape(experts, 2, data_ways, sliver // data_ways, model_width)
    sectioned_down = down_weight.reshape(experts, 1, data_ways, sliver // data_ways, model_width)
    sectioned_in = jnp.take(sectioned_in, slot_order, axis=0)
    sectioned_down = jnp.take(sectioned_down, slot_order, axis=0)
    relaid_in, relaid_down = (
        lax.all_to_all(
            lax.all_to_all(sectioned_in, "dp", split_axis=2, concat_axis=3, tiled=True),
            "expert",
            split_axis=0,
            concat_axis=3,
            tiled=True,
        ),
        lax.all_to_all(
            lax.all_to_all(sectioned_down, "dp", split_axis=2, concat_axis=3, tiled=True),
            "expert",
            split_axis=0,
            concat_axis=3,
            tiled=True,
        ),
    )
    full_in, full_down = (
        lax.all_gather(relaid_in, "dp", axis=3, tiled=True),
        lax.all_gather(relaid_down, "dp", axis=3, tiled=True),
    )
    pair_in = full_in.reshape(2, -1, model_width)
    pair_down = full_down.reshape(-1, model_width)
    group_rows = lax.all_gather(own_rows, "shard", axis=0, tiled=True)
    summed = lax.psum_scatter(
        jnp.dot(
            swiglu_rows(group_rows, pair_in), pair_down, preferred_element_type=jnp.float32
        ).astype(jnp.bfloat16),
        "shard",
        scatter_dimension=0,
        tiled=True,
    )
    returned = lax.all_to_all(
        summed.reshape(experts, capacity, model_width),
        "expert",
        split_axis=0,
        concat_axis=0,
        tiled=True,
    )
    combine_weights = jnp.sum(cell_hits * gate_values[:, :, None], axis=1)
    mixed_out = jnp.dot(
        combine_weights,
        returned.reshape(cell_count, model_width).astype(jnp.float32),
        precision=lax.Precision.HIGHEST,
    )
    return mixed_out.astype(jnp.bfloat16)


def solution(mesh):
    in_specs = (
        P(("dp", "expert", "shard"), None),
        P(None, None, ("dp", "expert", "shard"), None),
        P(None, ("dp", "expert", "shard"), None),
        P(("dp", "expert", "shard"), None),
        P(("dp", "expert", "shard"), None),
        P(("dp", "expert", "shard"), None),
        P(),
        P(),
    )
    out_specs = P(("dp", "expert", "shard"), None)
    return jax.shard_map(local, mesh=mesh, in_specs=in_specs, out_specs=out_specs, check_vma=False)
```

profile of v0, /device:TPU:8, one launch (start us, length us, event | category | flops | bytes accessed | tf_op | source)
XLA Modules:
  0.0 681.6 jit_solution(10519561180992360223)
XLA Ops:
  6.5 0.0 copy-start
  6.5 0.8 multiply_add_fusion
  7.4 0.9 convert_reduce_fusion
  8.3 1.2 convolution_convert_fusion.1
  9.5 0.9 reshape.64
  10.4 8.5 %all-to-all-start = ((bf16[8,4,6144]{2,1,0:T(4,128)(2,1)}), bf16[8,4,6144]{2,1,0:T(4,128)(2,1)S(1)}, u32[]{:S(2)}, u32[]{:S(2)}) async-start(bf16[8,4,6144]{2,1,0:T(4,128)(2,1)} %reshape.64), calls=%async_computation | async-start | bytes 786432 | tf_op jit(solution)/shard_map/all_to_all | solution.py:37
  18.8 0.9 select_reduce_fusion.1
  19.7 6.4 gather_fusion
  26.1 3.5 broadcast_select_fusion
  29.6 3.1 copy.24
  32.6 0.9 all-to-all-done
  33.5 6.3 all-to-all-start.1
  39.8 0.0 all-gather.4.cloned.1.call-start
  39.9 0.9 reshape.65
  40.7 0.0 all-gather.4.cloned.1.call-update
  40.8 0.0 all-gather.6.cloned.1.call-start
  40.8 89.5 %all-to-all-done.1 = bf16[8,2,2,16,6144]{4,3,1,0,2:T(8,128)(2,1)} async-done(((bf16[8,2,2,16,6144]{4,3,1,0,2:T(8,128)(2,1)}), bf16[8,2,2,16,6144]{4,3,1,0,2:T(8,128)(2,1)}, u32[]{:S(2)}, u32[]{:S(2)}) %all-to-all-start.1) | async-done | bytes 6291488 | tf_op jit(solution)/shard_map/all_to_all | solution.py:51
  130.3 3.5 copy.25
  133.8 145.8 %all_to_all.64 = bf16[8,2,1,32,6144]{4,3,1,2,0:T(8,128)(2,1)S(1)} all-to-all(bf16[8,2,1,32,6144]{4,3,1,2,0:T(8,128)(2,1)S(1)} %bitcast.37), channel_id=1, replica_groups=mesh['dp'=2,'expert'=8,'shard'=16] {'expert'}, dimensions={0} | all-to-all | bytes 12582912 | tf_op jit(solution)/shard_map/all_to_all | solution.py:50
  279.7 3.1 copy.27
  282.8 0.0 all-gather.6.cloned.1.call-update
  282.8 0.0 all-gather.8.cloned.1.call-start
  282.8 0.0 copy-done
  282.8 2.4 gather_fusion.1
  285.3 2.3 bitcast_select_fusion
  287.5 0.3 copy.28
  287.9 63.1 %all_to_all.65 = bf16[8,1,2,16,6144]{4,3,0,1,2:T(8,128)(2,1)S(1)} all-to-all(bf16[8,1,2,16,6144]{4,3,0,1,2:T(8,128)(2,1)S(1)} %copy.28), channel_id=1, replica_groups=mesh['dp'=2,'expert'=8,'shard'=16] {'dp'}, dimensions={2} | all-to-all | bytes 6291456 | tf_op jit(solution)/shard_map/all_to_all | solution.py:58
  350.9 0.3 copy.29
  351.2 66.1 %all_to_all.66 = bf16[8,1,1,32,6144]{4,3,2,1,0:T(8,128)(2,1)} all-to-all(bf16[8,1,1,32,6144]{4,3,2,1,0:T(8,128)(2,1)S(1)} %bitcast.40), channel_id=1, replica_groups=mesh['dp'=2,'expert'=8,'shard'=16] {'expert'}, dimensions={0} | all-to-all | bytes 6291456 | tf_op jit(solution)/shard_map/all_to_all | solution.py:57
  417.4 0.0 all-gather.8.cloned.1.call-update
  417.4 0.0 reduce-scatter.2.cloned.1.call-start
  417.5 0.0 all-gather.4.cloned.1.call-done
  417.5 41.2 %all-gather.6.cloned.1.call-done = bf16[1,2,1,512,6144]{4,3,1,2,0:T(8,128)(2,1)} async-done(((bf16[1,2,1,256,6144]{4,3,1,2,0:T(8,128)(2,1)}), bf16[1,2,1,512,6144]{4,3,1,2,0:T(8,128)(2,1)}) %all-gather.6.cloned.1.call-update) | async-done | bytes 12582928 | tf_op jit(solution)/shard_map/all_gather | solution.py:66
  458.6 12.5 %fusion = f32[512,2,512]{2,0,1:T(8,128)} fusion(bf16[1,2,1,512,6144]{4,3,1,2,0:T(8,128)(2,1)} %all-gather.6.cloned.1.call-done, bf16[512,6144]{1,0:T(8,128)(2,1)} %all-gather.4.cloned.1.call-done), kind=kOutput, calls=%fused_computation.2 | convolution fusion | flops 6442450944 | bytes 20971520 | tf_op jit(solution)/shard_map/rd,gud->rgu/dot_general | solution.py:14
  471.2 72.6 %all-gather.8.cloned.1.call-done = bf16[1,1,1,512,6144]{4,3,2,1,0:T(8,128)(2,1)} async-done(((bf16[1,1,1,256,6144]{4,3,2,1,0:T(8,128)(2,1)}), bf16[1,1,1,512,6144]{4,3,2,1,0:T(8,128)(2,1)}) %all-gather.8.cloned.1.call-update) | async-done | bytes 6291472 | tf_op jit(solution)/shard_map/all_gather | solution.py:67
  543.8 0.0 copy-start.1
  543.8 9.7 %convolution_convert_fusion = bf16[512,6144]{1,0:T(8,128)(2,1)} fusion(bf16[1,1,1,512,6144]{4,3,2,1,0:T(8,128)(2,1)} %all-gather.8.cloned.1.call-done, f32[512,2,512]{2,0,1:T(8,128)} %fusion), kind=kOutput, calls=%fused_computation.4 | convolution fusion | flops 3225944064 | bytes 14680064 | tf_op jit(solution)/shard_map/dot_general | solution.py:73
  553.5 0.0 reduce-scatter.2.cloned.1.call-update
  553.6 98.3 %reduce-scatter.2.cloned.1.call-done = bf16[32,6144]{1,0:T(8,128)(2,1)} async-done(((bf16[512,6144]{1,0:T(8,128)(2,1)}), bf16[32,6144]{1,0:T(8,128)(2,1)}) %reduce-scatter.2.cloned.1.call-update) | async-done | bytes 393232 | tf_op jit(solution)/shard_map/reduce_scatter | solution.py:72
  651.9 1.1 reshape.70
  653.0 20.0 %all_to_all.67 = bf16[8,4,6144]{2,1,0:T(4,128)(2,1)} all-to-all(bf16[8,4,6144]{2,1,0:T(4,128)(2,1)S(1)} %reshape.70), channel_id=1, replica_groups=mesh['dp'=2,'expert'=8,'shard'=16] {'expert'}, dimensions={0} | all-to-all | bytes 786432 | tf_op jit(solution)/shard_map/all_to_all | solution.py:80
  673.1 1.1 reshape.71
  674.1 0.9 convolution_convert_fusion.2
  675.1 0.0 copy-done.1
  (3 shorter events, 0.0 us)
Async XLA Ops:
  6.5 276.3 %copy-start = (bf16[8,32,6144]{2,1,0:T(8,128)(2,1)S(1)}, bf16[8,32,6144]{2,1,0:T(8,128)(2,1)}, u32[]{:S(2)}) copy-start(bf16[8,32,6144]{2,1,0:T(8,128)(2,1)} %param.10) | copy-start | bytes 9437188
  10.4 23.2 %all-to-all-start = ((bf16[8,4,6144]{2,1,0:T(4,128)(2,1)}), bf16[8,4,6144]{2,1,0:T(4,128)(2,1)S(1)}, u32[]{:S(2)}, u32[]{:S(2)}) async-start(bf16[8,4,6144]{2,1,0:T(4,128)(2,1)} %reshape.64), calls=%async_computation | async-start | bytes 786432 | tf_op jit(solution)/shard_map/all_to_all | solution.py:37
  33.5 96.8 %all-to-all-start.1 = ((bf16[8,2,2,16,6144]{4,3,1,0,2:T(8,128)(2,1)}), bf16[8,2,2,16,6144]{4,3,1,0,2:T(8,128)(2,1)}, u32[]{:S(2)}, u32[]{:S(2)}) async-start(bf16[8,2,2,16,6144]{4,3,1,0,2:T(8,128)(2,1)} %copy.24), calls=%async_computation.1 | async-start | bytes 12582912 | tf_op jit(solution)/shard_map/all_to_all | solution.py:51
  39.8 377.6 %all-gather.4.cloned.1.call-start = ((), (), s32[]{:S(2)}) async-start(), calls=%async_computation.7 | async-start | bytes 6684672 | tf_op jit(solution)/shard_map/all_gather | solution.py:71
  40.8 417.9 %all-gather.6.cloned.1.call-start = ((), (), s32[]{:S(2)}) async-start(), calls=%async_computation.8 | async-start | bytes 18874368 | tf_op jit(solution)/shard_map/all_gather | solution.py:66
  282.8 261.0 %all-gather.8.cloned.1.call-start = ((), (), s32[]{:S(2)}) async-start(), calls=%async_computation.9 | async-start | bytes 9437184 | tf_op jit(solution)/shard_map/all_gather | solution.py:67
  417.4 234.5 %reduce-scatter.2.cloned.1.call-start = ((), (), s32[]{:S(2)}) async-start(), calls=%async_computation.10 | async-start | bytes 6684672 | tf_op jit(solution)/shard_map/reduce_scatter | solution.py:72
  543.8 131.2 %copy-start.1 = (bf16[8,32,6144]{2,1,0:T(8,128)(2,1)S(1)}, bf16[8,32,6144]{2,1,0:T(8,128)(2,1)}, u32[]{:S(2)}) copy-start(bf16[8,32,6144]{2,1,0:T(8,128)(2,1)} %param.10) | copy-start | bytes 9437188
Sparse Core Ops, SparseCore 0:
  43.4 90.1 all-gather.3
  282.9 175.6 all-gather.5
  460.4 83.3 all-gather.7
  553.7 98.1 reduce-scatter.1
where the time goes:
time: 682 us
  waiting for transfers between devices  303 us (44%)
  blocking collectives  295 us (43%)
  matrix products  24.3 us (4%)
  local copies, waits for them, and re-layouts  23.1 us (3%)
  starting transfers between devices  15 us (2%)
  between operations  13.2 us (2%)
  other arithmetic  8.31 us (1%)
    all_to_all x1, blocking collectives, local(): lax.all_to_all(lax.all_to_all(sectioned_in, 'dp', split_axis=2, concat_ax...  146 us
    reduce_scatter x1, waiting for transfers between devices, local(): lax.psum_scatter(jnp.dot(swiglu_rows(group_rows, pair_in), pair_down, pre...  98.3 us
    all_to_all x1, waiting for transfers between devices, local(): lax.all_to_all(sectioned_in, 'dp', split_axis=2, concat_axis=3, tiled=True)  89.5 us
    all_gather x1, waiting for transfers between devices, local(): lax.all_gather(relaid_down, 'dp', axis=3, tiled=True)  72.6 us
    all_to_all x1, blocking collectives, local(): lax.all_to_all(lax.all_to_all(sectioned_down, 'dp', split_axis=2, concat_...  66.1 us
    all_to_all x1, blocking collectives, local(): lax.all_to_all(sectioned_down, 'dp', split_axis=2, concat_axis=3, tiled=T...  63.1 us
    all_gather x1, waiting for transfers between devices, local(): lax.all_gather(relaid_in, 'dp', axis=3, tiled=True)  41.2 us
    all_to_all x1, blocking collectives, local(): lax.all_to_all(summed.reshape(experts, capacity, model_width), 'expert',...  20 us
  transfers between devices with their start and end apart: 6, of which 5 were waited for; matrix products, arithmetic and copies ran while one was open for 6% of the time, Pallas kernels for 0%

commit v1 on v0

--- a/solution.py
+++ b/solution.py
@@ -54,12 +54,22 @@
             concat_axis=3,
             tiled=True,
         ),
-        lax.all_to_all(
-            lax.all_to_all(sectioned_down, "dp", split_axis=2, concat_axis=3, tiled=True),
-            "expert",
-            split_axis=0,
-            concat_axis=3,
-            tiled=True,
+        jnp.concatenate(
+            lax.all_to_all(
+                jnp.stack(
+                    jnp.split(
+                        lax.all_to_all(
+                            sectioned_down, "dp", split_axis=2, concat_axis=3, tiled=True
+                        ),
+                        lax.axis_size("expert"),
+                        axis=0,
+                    )
+                ),
+                "expert",
+                0,
+                0,
+            ),
+            axis=3,
         ),
     )
     full_in, full_down = (

time: 682 us -> 659 us (0.966)
  blocking collectives: 295 us -> 94.4 us
  waiting for transfers between devices: 303 us -> 467 us
  starting transfers between devices: 15 us -> 23.8 us
  local copies, waits for them, and re-layouts: 23.1 us -> 30.8 us
    all_to_all x3 -> x1, blocking collectives: 275 us -> 74.5 us  [local(): lax.all_to_all(jnp.stack(jnp.split(lax.all_to_all(sectioned_down, 'dp', s...]
    all_to_all x0 -> x2, waiting for transfers between devices: none -> 174 us  [the longest x1 131 us: local(): lax.all_to_all(lax.all_to_all(sectioned_in, 'dp', split_axis=2, concat_ax...]
    all_to_all x1, waiting for transfers between devices: 89.5 us -> 67.9 us  [local(): lax.all_to_all(sectioned_in, 'dp', split_axis=2, concat_axis=3, tiled=True)]
    all_to_all x0 -> x2, starting transfers between devices: none -> 8.71 us  [the longest x1 4.77 us: local(): lax.all_to_all(lax.all_to_all(sectioned_in, 'dp', split_axis=2, concat_ax...]
  transfers between devices with their start and end apart: 6 -> 8, of which waited for: 5 -> 7; matrix products, arithmetic and copies ran while one was open for 6% -> 5% of each run, Pallas kernels for 0% -> 0%
where the time goes in v1:
time: 659 us; the launch traced here: 658 us
  waiting for transfers between devices  467 us (71%)
  blocking collectives  94.4 us (14%)
  local copies, waits for them, and re-layouts  30.8 us (5%)
  starting transfers between devices  23.8 us (4%)
  matrix products  21.8 us (3%)
  between operations  13.3 us (2%)
  other arithmetic  6.81 us (1%)
    all_to_all x1, waiting for transfers between devices, local(): lax.all_to_all(lax.all_to_all(sectioned_in, 'dp', split_axis=2, concat_ax...  131 us
    reduce_scatter x1, waiting for transfers between devices, local(): lax.psum_scatter(jnp.dot(swiglu_rows(group_rows, pair_in), pair_down, pre...  98.4 us
    all_to_all x1, blocking collectives, local(): lax.all_to_all(jnp.stack(jnp.split(lax.all_to_all(sectioned_down, 'dp', s...  74.5 us
    all_gather x1, waiting for transfers between devices, local(): lax.all_gather(relaid_down, 'dp', axis=3, tiled=True)  71.9 us
    all_to_all x1, waiting for transfers between devices, local(): lax.all_to_all(sectioned_in, 'dp', split_axis=2, concat_axis=3, tiled=True)  67.9 us
    all_gather x1, waiting for transfers between devices, local(): lax.all_gather(relaid_in, 'dp', axis=3, tiled=True)  47.3 us
    all_to_all x1, waiting for transfers between devices, local(): lax.all_to_all(sectioned_down, 'dp', split_axis=2, concat_axis=3, tiled=T...  42.8 us
    all_to_all x1, blocking collectives, local(): lax.all_to_all(summed.reshape(experts, capacity, model_width), 'expert',...  20 us
  transfers between devices with their start and end apart: 8, of which 7 were waited for; matrix products, arithmetic and copies ran while one was open for 5% of the time, Pallas kernels for 0%

profile of v1, /device:TPU:8, one launch (start us, length us, event | category | flops | bytes accessed | tf_op | source)
XLA Modules:
  0.0 658.4 jit_solution(901327273945168936)
XLA Ops:
  6.5 0.0 copy-start
  6.5 1.0 select_reduce_fusion.1
  7.6 6.4 gather_fusion
  14.0 3.5 broadcast_select_fusion
  17.4 3.1 copy.22
  20.5 0.0 copy-start.2
  20.5 0.0 copy-start.3
  20.5 0.0 copy-start.4
  20.5 6.5 all-to-all-start.1
  27.0 0.0 copy-done.2
  27.0 0.0 copy-done.3
  27.0 0.0 copy-done.4
  27.0 0.1 convert_reduce_fusion
  27.1 1.2 convolution_convert_fusion.1
  28.3 0.9 reshape.82
  29.2 67.9 %all-to-all-done.1 = bf16[8,2,2,16,6144]{4,3,1,0,2:T(8,128)(2,1)} async-done(((bf16[8,2,2,16,6144]{4,3,1,0,2:T(8,128)(2,1)}), bf16[8,2,2,16,6144]{4,3,1,0,2:T(8,128)(2,1)}, u32[]{:S(2)}, u32[]{:S(2)}) %all-to-all-start.1) | async-done | bytes 6291488 | tf_op jit(solution)/shard_map/all_to_all | solution.py:51
  97.1 8.5 %all-to-all-start = ((bf16[8,4,6144]{2,1,0:T(4,128)(2,1)}), bf16[8,4,6144]{2,1,0:T(4,128)(2,1)S(1)}, u32[]{:S(2)}, u32[]{:S(2)}) async-start(bf16[8,4,6144]{2,1,0:T(4,128)(2,1)} %reshape.82), calls=%async_computation | async-start | bytes 786432 | tf_op jit(solution)/shard_map/all_to_all | solution.py:37
  105.6 6.2 copy.23
  111.8 7.6 %all-to-all-done = bf16[8,4,6144]{2,1,0:T(4,128)(2,1)S(1)} async-done(((bf16[8,4,6144]{2,1,0:T(4,128)(2,1)}), bf16[8,4,6144]{2,1,0:T(4,128)(2,1)S(1)}, u32[]{:S(2)}, u32[]{:S(2)}) %all-to-all-start) | async-done | bytes 393248 | tf_op jit(solution)/shard_map/all_to_all | solution.py:37
  119.4 4.8 all-to-all-start.2
  124.2 0.0 all-gather.4.cloned.1.call-start
  124.2 0.9 reshape.83
  125.1 0.0 all-gather.4.cloned.1.call-update
  125.1 0.0 copy-done
  125.1 2.4 gather_fusion.1
  127.6 2.3 bitcast_select_fusion
  129.8 2.0 copy.26
  131.8 131.4 %all-to-all-done.2 = bf16[8,2,1,32,6144]{4,3,1,2,0:T(8,128)(2,1)} async-done(((bf16[8,2,1,32,6144]{4,3,1,2,0:T(8,128)(2,1)}), bf16[8,2,1,32,6144]{4,3,1,2,0:T(8,128)(2,1)}, u32[]{:S(2)}, u32[]{:S(2)}) %all-to-all-start.2) | async-done | bytes 6291488 | tf_op jit(solution)/shard_map/all_to_all | solution.py:50
  263.3 3.9 all-to-all-start.3
  267.2 0.0 all-gather.6.cloned.1.call-start
  267.3 6.2 copy.25
  273.5 0.0 all-gather.6.cloned.1.call-update
  273.5 0.0 all-gather.8.cloned.1.call-start
  273.6 42.8 %all-to-all-done.3 = bf16[8,1,2,16,6144]{4,3,0,1,2:T(8,128)(2,1)S(1)} async-done(((bf16[8,1,2,16,6144]{4,3,0,1,2:T(8,128)(2,1)}), bf16[8,1,2,16,6144]{4,3,0,1,2:T(8,128)(2,1)S(1)}, u32[]{:S(2)}, u32[]{:S(2)}) %all-to-all-start.3) | async-done | bytes 3145760 | tf_op jit(solution)/shard_map/all_to_all | solution.py:61
  316.4 0.2 fusion.10
  316.9 74.5 %all_to_all.54 = bf16[8,1,1,1,32,6144]{5,4,3,2,1,0:T(8,128)(2,1)} all-to-all(bf16[8,1,1,1,32,6144]{5,4,3,2,1,0:T(8,128)(2,1)S(1)} %constant_dynamic-update-slice_fusion), channel_id=1, replica_groups=mesh['dp'=2,'expert'=8,'shard'=16] {'expert'}, dimensions={0} | all-to-all | bytes 6291456 | tf_op jit(solution)/shard_map/all_to_all | solution.py:58
  391.3 0.0 all-gather.8.cloned.1.call-update
  391.3 0.0 reduce-scatter.2.cloned.1.call-start
  391.4 0.0 all-gather.4.cloned.1.call-done
  391.4 47.3 %all-gather.6.cloned.1.call-done = bf16[1,2,1,512,6144]{4,3,1,2,0:T(8,128)(2,1)} async-done(((bf16[1,2,1,256,6144]{4,3,1,2,0:T(8,128)(2,1)}), bf16[1,2,1,512,6144]{4,3,1,2,0:T(8,128)(2,1)}) %all-gather.6.cloned.1.call-update) | async-done | bytes 12582928 | tf_op jit(solution)/shard_map/all_gather | solution.py:76
  438.7 11.6 %fusion = f32[512,2,512]{2,0,1:T(8,128)S(1)} fusion(bf16[1,2,1,512,6144]{4,3,1,2,0:T(8,128)(2,1)} %all-gather.6.cloned.1.call-done, bf16[512,6144]{1,0:T(8,128)(2,1)} %all-gather.4.cloned.1.call-done), kind=kOutput, calls=%fused_computation.2 | convolution fusion | flops 6442450944 | bytes 20971520 | tf_op jit(solution)/shard_map/rd,gud->rgu/dot_general | solution.py:14
  450.3 71.9 %all-gather.8.cloned.1.call-done = bf16[1,1,1,512,6144]{4,3,2,1,0:T(8,128)(2,1)} async-done(((bf16[1,1,1,256,6144]{4,3,2,1,0:T(8,128)(2,1)}), bf16[1,1,1,512,6144]{4,3,2,1,0:T(8,128)(2,1)}) %all-gather.8.cloned.1.call-update) | async-done | bytes 6291472 | tf_op jit(solution)/shard_map/all_gather | solution.py:77
  522.2 8.1 %convolution_convert_fusion = bf16[512,6144]{1,0:T(8,128)(2,1)} fusion(bf16[1,1,1,512,6144]{4,3,2,1,0:T(8,128)(2,1)} %all-gather.8.cloned.1.call-done, f32[512,2,512]{2,0,1:T(8,128)S(1)} %fusion), kind=kOutput, calls=%fused_computation.4 | convolution fusion | flops 3225944064 | bytes 14680064 | tf_op jit(solution)/shard_map/dot_general | solution.py:83
  530.4 0.0 copy-start.1
  530.4 0.0 reduce-scatter.2.cloned.1.call-update
  530.4 98.4 %reduce-scatter.2.cloned.1.call-done = bf16[32,6144]{1,0:T(8,128)(2,1)} async-done(((bf16[512,6144]{1,0:T(8,128)(2,1)}), bf16[32,6144]{1,0:T(8,128)(2,1)}) %reduce-scatter.2.cloned.1.call-update) | async-done | bytes 393232 | tf_op jit(solution)/shard_map/reduce_scatter | solution.py:82
  628.8 1.1 reshape.89
  629.9 20.0 %all_to_all.55 = bf16[8,4,6144]{2,1,0:T(4,128)(2,1)} all-to-all(bf16[8,4,6144]{2,1,0:T(4,128)(2,1)S(1)} %reshape.89), channel_id=1, replica_groups=mesh['dp'=2,'expert'=8,'shard'=16] {'expert'}, dimensions={0} | all-to-all | bytes 786432 | tf_op jit(solution)/shard_map/all_to_all | solution.py:90
  649.9 1.1 reshape.90
  651.0 0.9 convolution_convert_fusion.2
  651.9 0.0 copy-done.1
  (12 shorter events, 0.2 us)
Async XLA Ops:
  6.5 118.6 %copy-start = (bf16[8,32,6144]{2,1,0:T(8,128)(2,1)S(1)}, bf16[8,32,6144]{2,1,0:T(8,128)(2,1)}, u32[]{:S(2)}) copy-start(bf16[8,32,6144]{2,1,0:T(8,128)(2,1)} %param.10) | copy-start | bytes 9437188
  20.5 6.5 copy-start.2
  20.5 6.5 copy-start.3
  20.5 6.5 copy-start.4
  20.5 76.6 %all-to-all-start.1 = ((bf16[8,2,2,16,6144]{4,3,1,0,2:T(8,128)(2,1)}), bf16[8,2,2,16,6144]{4,3,1,0,2:T(8,128)(2,1)}, u32[]{:S(2)}, u32[]{:S(2)}) async-start(bf16[8,2,2,16,6144]{4,3,1,0,2:T(8,128)(2,1)} %copy.22), calls=%async_computation.1 | async-start | bytes 12582912 | tf_op jit(solution)/shard_map/all_to_all | solution.py:51
  97.1 22.3 %all-to-all-start = ((bf16[8,4,6144]{2,1,0:T(4,128)(2,1)}), bf16[8,4,6144]{2,1,0:T(4,128)(2,1)S(1)}, u32[]{:S(2)}, u32[]{:S(2)}) async-start(bf16[8,4,6144]{2,1,0:T(4,128)(2,1)} %reshape.82), calls=%async_computation | async-start | bytes 786432 | tf_op jit(solution)/shard_map/all_to_all | solution.py:37
  119.4 143.9 %all-to-all-start.2 = ((bf16[8,2,1,32,6144]{4,3,1,2,0:T(8,128)(2,1)}), bf16[8,2,1,32,6144]{4,3,1,2,0:T(8,128)(2,1)}, u32[]{:S(2)}, u32[]{:S(2)}) async-start(bf16[8,2,1,32,6144]{4,3,1,2,0:T(8,128)(2,1)} %bitcast.42), calls=%async_computation.2 | async-start | bytes 12582912 | tf_op jit(solution)/shard_map/all_to_all | solution.py:50
  124.2 267.2 %all-gather.4.cloned.1.call-start = ((), (), s32[]{:S(2)}) async-start(), calls=%async_computation.7 | async-start | bytes 6684672 | tf_op jit(solution)/shard_map/all_gather | solution.py:81
  263.3 53.1 %all-to-all-start.3 = ((bf16[8,1,2,16,6144]{4,3,0,1,2:T(8,128)(2,1)}), bf16[8,1,2,16,6144]{4,3,0,1,2:T(8,128)(2,1)S(1)}, u32[]{:S(2)}, u32[]{:S(2)}) async-start(bf16[8,1,2,16,6144]{4,3,0,1,2:T(8,128)(2,1)} %copy.26), calls=%async_computation.3 | async-start | bytes 6291456 | tf_op jit(solution)/shard_map/all_to_all | solution.py:61
  267.2 171.5 %all-gather.6.cloned.1.call-start = ((), (), s32[]{:S(2)}) async-start(), calls=%async_computation.8 | async-start | bytes 18874368 | tf_op jit(solution)/shard_map/all_gather | solution.py:76
  273.5 248.7 %all-gather.8.cloned.1.call-start = ((), (), s32[]{:S(2)}) async-start(), calls=%async_computation.9 | async-start | bytes 9437184 | tf_op jit(solution)/shard_map/all_gather | solution.py:77
  391.3 237.4 %reduce-scatter.2.cloned.1.call-start = ((), (), s32[]{:S(2)}) async-start(), calls=%async_computation.10 | async-start | bytes 6684672 | tf_op jit(solution)/shard_map/reduce_scatter | solution.py:82
  530.4 121.5 %copy-start.1 = (bf16[8,32,6144]{2,1,0:T(8,128)(2,1)S(1)}, bf16[8,32,6144]{2,1,0:T(8,128)(2,1)}, u32[]{:S(2)}) copy-start(bf16[8,32,6144]{2,1,0:T(8,128)(2,1)} %param.10) | copy-start | bytes 9437188
Sparse Core Ops, SparseCore 0:
  127.8 68.8 all-gather.3
  273.6 165.0 all-gather.5
  440.5 81.6 all-gather.7
  530.5 98.1 reduce-scatter.1
